TPU v7x, 512 devices: a whole 4x8x8 slice. The times are simulated.
512 devices in a mesh: tile: 32 (over y, x), ir: 16 (over z, core).
Axes of the slice: x: 4, y: 8, z: 8, core: 2. Of those that a mesh axis runs over, the one named last changes fastest.
Arguments:
- samples: bfloat16 [4096, 1024], P(('tile', 'ir')), may hold values from -6 to 6
- ir_spectra: bfloat16 [16, 128, 2, 1024], P(None, 'ir'), may hold values from -0.5 to 0.5
- clip_lengths: int32 [16], replicated, may hold values from 1 to 1024, 4096 in all
- room_ids: int32 [16], replicated, may hold values from 0 to 15
Outputs:
- filtered: float32 [4096, 1024], P(('tile', 'ir'))
Inputs may be any that keep to these rules, and one draw needn't show every extreme that they name: `clip_lengths`: the lengths sum to 4096; clips lie end to end in block order.
All inputs are finite; a program needn't handle non-finite values.
Results may differ from a plain program's by a relative error of at most 0.0037.
Values may be sent and summed in bfloat16 or wider, within the bound.
A program may use at most 128 MiB of HBM per device.

v0:
```python
import jax
import jax.numpy as jnp
import numpy as np
from jax import lax
from jax.sharding import PartitionSpec as P


def from_behind(x, axis, by):
    length = lax.axis_size(axis)
    pairs = [(i, i + by) for i in range(length) if 0 <= i + by < length]
    return lax.ppermute(x, axis, pairs)


def in_blocks(x, dim, length):
    before, after = (x.shape[:dim], x.shape[dim + 1 :])
    return jnp.moveaxis(x.reshape(*before, length, -1, *after), dim, 0)


def sent_and_summed(x, axis, dim):
    tiles = in_blocks(x, dim, lax.axis_size(axis))
    arrived = lax.all_to_all(tiles, axis, split_axis=0, concat_axis=0, tiled=True)
    return arrived.sum(axis=0)


def forward_table(width):
    length = 2 * width
    sample = np.arange(length)
    bins = np.arange(width)
    phase = sample[:, None] * bins[None, :] % length
    angle = phase * (2.0 * np.pi / length)
    parity = np.where(sample % 2 == 0, 1.0, -1.0)
    sines = np.where(bins[None, :] == 0, parity[:, None], -np.sin(angle))
    table = np.concatenate([np.cos(angle), sines], axis=1)
    return jnp.asarray(table, dtype=jnp.float32).astype(jnp.bfloat16)


def inverse_table(width):
    length = 2 * width
    bins = np.arange(width)
    outputs = width + np.arange(width)
    phase = bins[:, None] * outputs[None, :] % length
    angle = phase * (2.0 * np.pi / length)
    weight = np.where(bins == 0, 1.0, 2.0)[:, None] / length
    parity = np.where(outputs % 2 == 0, 1.0, -1.0)[None, :] / length
    cosines = weight * np.cos(angle)
    sines = np.where(bins[:, None] == 0, parity, -weight * np.sin(angle))
    table = np.concatenate([cosines, sines], axis=0)
    return jnp.asarray(table, dtype=jnp.float32)


def packed_product(spectrum, response, width):
    are, aim = (spectrum[:, :width], spectrum[:, width:])
    hre, him = (response[:, :width], response[:, width:])
    cross = (jnp.arange(width, dtype=jnp.int32) > 0).astype(jnp.float32)[None, :]
    real = are * hre - cross * aim * him
    imag = cross * (are * him + aim * hre) + (1.0 - cross) * aim * him
    return jnp.concatenate([real, imag], axis=1)


def clip_info(clip_lengths, room_ids, blocks):
    ends = jnp.cumsum(clip_lengths)
    starts = ends - clip_lengths
    member = (blocks[:, None] >= starts[None, :]) & (blocks[:, None] < ends[None, :])
    begin = jnp.sum(jnp.where(member, starts[None, :], 0), axis=1)
    room = jnp.sum(jnp.where(member, room_ids[None, :], 0), axis=1)
    return (begin, room)


def on_device(samples, ir_spectra, clip_lengths, room_ids):
    rows, width = samples.shape
    groups = lax.axis_size("ir")
    count = rows * groups
    rooms, part_dev = (ir_spectra.shape[0], ir_spectra.shape[1])
    parts = part_dev * groups
    tile_base = lax.axis_index("tile") * count
    own_blocks = tile_base + lax.axis_index("ir") * rows + jnp.arange(rows, dtype=jnp.int32)
    own_begin, own_room = clip_info(clip_lengths, room_ids, own_blocks)
    before = from_behind(samples[rows - 1 :], ("tile", "ir"), 1)
    earlier = jnp.concatenate([before, samples[:-1]], axis=0)
    earlier = jnp.where((own_blocks == own_begin)[:, None], jnp.zeros_like(earlier), earlier)
    frames = jnp.concatenate([earlier, samples], axis=1)
    own_spectra = jnp.dot(frames, forward_table(width), preferred_element_type=jnp.float32).astype(
        jnp.bfloat16
    )
    blocks = tile_base + jnp.arange(count, dtype=jnp.int32)
    begin, room = clip_info(clip_lengths, room_ids, blocks)
    room_hot = (room[:, None] == jnp.arange(rooms, dtype=jnp.int32)[None, :]).astype(jnp.bfloat16)
    inverse = inverse_table(width)
    spectra = lax.all_gather(own_spectra, "ir", axis=0, tiled=True)
    delayed = from_behind(spectra[count - (parts - 1) :], "tile", 1)
    padded = jnp.concatenate([delayed, spectra], axis=0)
    flat_filters = ir_spectra.reshape(rooms, part_dev * 2 * width)
    selected = jnp.dot(room_hot, flat_filters, preferred_element_type=jnp.float32).astype(
        jnp.bfloat16
    )
    selected = selected.reshape(count, part_dev, 2 * width)
    first = lax.axis_index("ir") * part_dev

    def add_partition(index, summed):
        delay = first + index
        moved = lax.dynamic_slice_in_dim(padded, parts - 1 - delay, count, 0)
        chosen = lax.dynamic_index_in_dim(selected, index, 1, keepdims=False)
        live = blocks - delay >= begin
        term = packed_product(moved.astype(jnp.float32), chosen.astype(jnp.float32), width)
        return summed + jnp.where(live[:, None], term, jnp.zeros_like(term))

    summed = lax.fori_loop(0, part_dev, add_partition, jnp.zeros((count, 2 * width), jnp.float32))
    return sent_and_summed(
        jnp.dot(
            summed, inverse, precision=lax.Precision.HIGHEST, preferred_element_type=jnp.float32
        ),
        "ir",
        0,
    )


def solution(mesh):
    in_specs = (P(("tile", "ir"), None), P(None, "ir", None, None), P(), P())
    out_specs = P(("tile", "ir"), None)
    return jax.shard_map(
        on_device, mesh=mesh, in_specs=in_specs, out_specs=out_specs, check_vma=False
    )
```

profile of v0, /device:TPU:33, one launch (start us, length us, event | category | flops | bytes accessed | tf_op | source)
XLA Modules:
  0.0 97.9 jit_solution(4870245839410674996)
XLA Ops:
  0.0 0.8 slice.49
  0.8 4.5 %collective-permute-start = (bf16[1,1024]{1,0:T(2,128)(2,1)S(1)}, bf16[1,1024]{1,0:T(2,128)(2,1)S(1)}, u32[]{:S(2)}, u32[]{:S(2)}) collective-permute-start(bf16[1,1024]{1,0:T(2,128)(2,1)S(1)} %slice.49), channel_id=1, source_target_pairs={{0,1},{1,2},{2,3},{3,4},{4,5},{5,6},{6,7},{7,8},{8,9},{9,10},{10,1... | collective-permute-start | bytes 6152 | tf_op jit(solution)/shard_map/ppermute | solution.py:11
  5.4 0.7 copy.11
  6.3 0.7 sub.58
  6.9 2.8 %convolution_bitcast_fusion = f32[8,2048]{1,0:T(8,128)S(1)} fusion(bf16[1024,2048]{1,0:T(8,128)(2,1)} %constant.107, bf16[8,1024]{1,0:T(8,128)(2,1)} %param.8), kind=kOutput, calls=%fused_computation.14 | convolution fusion | flops 33554432 | bytes 4276224 | tf_op jit(solution)/shard_map/dot_general | solution.py:82
  10.0 0.4 reshape.73
  10.4 2.9 %fusion.5 = bf16[8,2048]{1,0:T(8,128)(2,1)S(1)} fusion(f32[8,2048]{1,0:T(8,128)S(1)} %convolution_bitcast_fusion, bf16[1024,2048]{1,0:T(8,128)(2,1)} %constant.106, bf16[7,1024]{1,0:T(8,128)(2,1)S(1)} %bitcast.23, bf16[1,1024]{1,0:T(2,128)(2,1)S(1)} %collective-permute-done, pred[8]{0:T(512)(128)(4,1)S(1)} %fusion.13), kind=kOutput, calls=%fused_computation.16 | convolution fusion | flops 33628160 | bytes 4309000 | tf_op jit(solution)/shard_map/dot_general | solution.py:82
  13.3 22.5 %all_gather.3 = bf16[128,2048]{1,0:T(8,128)(2,1)S(1)} all-gather(bf16[8,2048]{1,0:T(8,128)(2,1)S(1)} %fusion.5), channel_id=1, replica_groups=mesh['tile'=32,'ir'=16] {'ir'}, dimensions={0}, use_global_device_ids=true | all-gather | bytes 557056 | tf_op jit(solution)/shard_map/all_gather | solution.py:89
  35.9 3.1 %collective-permute-start.1 = (bf16[127,2048]{1,0:T(8,128)(2,1)S(1)}, bf16[127,2048]{1,0:T(8,128)(2,1)S(1)}, u32[]{:S(2)}, u32[]{:S(2)}) collective-permute-start(bf16[127,2048]{1,0:T(8,128)(2,1)S(1)} %slice.62), channel_id=1, source_target_pairs={{0,16},{16,32},{32,48},{48,64},{64,80},{80,96},{96,112},{112,128},... | collective-permute-start | bytes 1560584 | tf_op jit(solution)/shard_map/ppermute | solution.py:11
  39.1 1.3 %convolution_convert_fusion = bf16[128,16384]{1,0:T(8,128)(2,1)S(1)} fusion(bf16[16,16384]{1,0:T(8,128)(2,1)S(1)} %reshape.73, s32[128]{0:T(128)S(1)} %get-tuple-element.230), kind=kOutput, calls=%fused_computation.12 | convolution fusion | flops 69208064 | bytes 4719104 | tf_op jit(solution)/shard_map/dot_general | solution.py:93
  40.4 2.2 %copy.15 = bf16[16,8,8,2048]{3,2,0,1:T(8,128)(2,1)} copy(bf16[16,8,8,2048]{3,2,1,0:T(8,128)(2,1)S(1)} %bitcast.21) | data formatting | bytes 8388608 | tf_op jit(solution)/shard_map/reshape | solution.py:96
  42.6 11.8 %collective-permute-done.1 = bf16[127,2048]{1,0:T(8,128)(2,1)S(1)} collective-permute-done((bf16[127,2048]{1,0:T(8,128)(2,1)S(1)}, bf16[127,2048]{1,0:T(8,128)(2,1)S(1)}, u32[]{:S(2)}, u32[]{:S(2)}) %collective-permute-start.1) | collective-permute-done | bytes 520224 | tf_op jit(solution)/shard_map/ppermute | solution.py:11
  54.5 14.4 %while.16 = (s32[]{:T(128)}, f32[128,2048]{1,0:T(8,128)S(1)}, s32[]{:T(128)}, s32[128]{0:T(128)S(1)}, bf16[255,2048]{1,0:T(8,128)(2,1)S(1)}, /*index=5*/bf16[128...) while((s32[]{:T(128)}, f32[128,2048]{1,0:T(8,128)S(1)}, ...), condition=%wide.region_5.6_spmd.clone, body=%wide.region_4.5_spmd.clone.sunk | while | flops 3020168 | bytes 9454529 | solution.py:107
  54.7 1.1 %bitcast_convert_fusion.2 = f32[128,2048]{1,0:T(8,128)S(1)} fusion(bf16[128,8,2048]{2,0,1:T(8,128)(2,1)} %get-tuple-element.322, s32[]{:T(128)} %get-tuple-element.306), kind=kLoop, calls=%fused_computation.3.clone.1 | loop fusion | flops 262144 | bytes 1572868 | tf_op jit(solution)/shard_map/while/body/eval_jaxpr/convert_element_type | solution.py:104
  56.5 1.1 %bitcast_convert_fusion.2 = f32[128,2048]{1,0:T(8,128)S(1)} fusion(bf16[128,8,2048]{2,0,1:T(8,128)(2,1)} %get-tuple-element.322, s32[]{:T(128)} %get-tuple-element.306), kind=kLoop, calls=%fused_computation.3.clone.1 | loop fusion | flops 262144 | bytes 1572868 | tf_op jit(solution)/shard_map/while/body/eval_jaxpr/convert_element_type | solution.py:104
  58.3 1.1 %bitcast_convert_fusion.2 = f32[128,2048]{1,0:T(8,128)S(1)} fusion(bf16[128,8,2048]{2,0,1:T(8,128)(2,1)} %get-tuple-element.322, s32[]{:T(128)} %get-tuple-element.306), kind=kLoop, calls=%fused_computation.3.clone.1 | loop fusion | flops 262144 | bytes 1572868 | tf_op jit(solution)/shard_map/while/body/eval_jaxpr/convert_element_type | solution.py:104
  60.1 1.1 %bitcast_convert_fusion.2 = f32[128,2048]{1,0:T(8,128)S(1)} fusion(bf16[128,8,2048]{2,0,1:T(8,128)(2,1)} %get-tuple-element.322, s32[]{:T(128)} %get-tuple-element.306), kind=kLoop, calls=%fused_computation.3.clone.1 | loop fusion | flops 262144 | bytes 1572868 | tf_op jit(solution)/shard_map/while/body/eval_jaxpr/convert_element_type | solution.py:104
  61.9 1.1 %bitcast_convert_fusion.2 = f32[128,2048]{1,0:T(8,128)S(1)} fusion(bf16[128,8,2048]{2,0,1:T(8,128)(2,1)} %get-tuple-element.322, s32[]{:T(128)} %get-tuple-element.306), kind=kLoop, calls=%fused_computation.3.clone.1 | loop fusion | flops 262144 | bytes 1572868 | tf_op jit(solution)/shard_map/while/body/eval_jaxpr/convert_element_type | solution.py:104
  63.7 1.1 %bitcast_convert_fusion.2 = f32[128,2048]{1,0:T(8,128)S(1)} fusion(bf16[128,8,2048]{2,0,1:T(8,128)(2,1)} %get-tuple-element.322, s32[]{:T(128)} %get-tuple-element.306), kind=kLoop, calls=%fused_computation.3.clone.1 | loop fusion | flops 262144 | bytes 1572868 | tf_op jit(solution)/shard_map/while/body/eval_jaxpr/convert_element_type | solution.py:104
  65.5 1.1 %bitcast_convert_fusion.2 = f32[128,2048]{1,0:T(8,128)S(1)} fusion(bf16[128,8,2048]{2,0,1:T(8,128)(2,1)} %get-tuple-element.322, s32[]{:T(128)} %get-tuple-element.306), kind=kLoop, calls=%fused_computation.3.clone.1 | loop fusion | flops 262144 | bytes 1572868 | tf_op jit(solution)/shard_map/while/body/eval_jaxpr/convert_element_type | solution.py:104
  67.3 1.1 %bitcast_convert_fusion.2 = f32[128,2048]{1,0:T(8,128)S(1)} fusion(bf16[128,8,2048]{2,0,1:T(8,128)(2,1)} %get-tuple-element.322, s32[]{:T(128)} %get-tuple-element.306), kind=kLoop, calls=%fused_computation.3.clone.1 | loop fusion | flops 262144 | bytes 1572868 | tf_op jit(solution)/shard_map/while/body/eval_jaxpr/convert_element_type | solution.py:104
  68.9 7.2 %convolution_bitcast_fusion.1 = f32[16,8,1024]{2,1,0:T(8,128)S(1)} fusion(f32[128,2048]{1,0:T(8,128)S(1)} %get-tuple-element.181, f32[2048,1024]{1,0:T(8,128)} %constant.102.clone), kind=kOutput, calls=%fused_computation.17 | convolution fusion | flops 3221225472 | bytes 9961472 | tf_op jit(solution)/shard_map/dot_general | solution.py:109
  76.2 21.1 %all_to_all.5 = f32[16,8,1024]{2,1,0:T(8,128)S(1)} all-to-all(f32[16,8,1024]{2,1,0:T(8,128)S(1)} %convolution_bitcast_fusion.1), channel_id=1, replica_groups=mesh['tile'=32,'ir'=16] {'ir'}, dimensions={0} | all-to-all | bytes 1048576 | tf_op jit(solution)/shard_map/all_to_all | solution.py:21
  97.3 0.6 reduce_sum.39
  (65 shorter events, 5.4 us)
Async XLA Ops:
  0.0 10.4 %copy-start.1 = (bf16[8,1024]{1,0:T(8,128)(2,1)S(1)}, bf16[8,1024]{1,0:T(8,128)(2,1)}, u32[]{:S(2)}) copy-start(bf16[8,1024]{1,0:T(8,128)(2,1)} %param.8) | copy-start | bytes 49156
  0.0 10.0 %copy-start = (bf16[16,8,2,1024]{3,2,1,0:T(2,128)(2,1)S(1)}, bf16[16,8,2,1024]{3,2,1,0:T(2,128)(2,1)}, u32[]{:S(2)}) copy-start(bf16[16,8,2,1024]{3,2,1,0:T(2,128)(2,1)} %param.9) | copy-start | bytes 1572868
  0.8 9.6 %collective-permute-start = (bf16[1,1024]{1,0:T(2,128)(2,1)S(1)}, bf16[1,1024]{1,0:T(2,128)(2,1)S(1)}, u32[]{:S(2)}, u32[]{:S(2)}) collective-permute-start(bf16[1,1024]{1,0:T(2,128)(2,1)S(1)} %slice.49), channel_id=1, source_target_pairs={{0,1},{1,2},{2,3},{3,4},{4,5},{5,6},{6,7},{7,8},{8,9},{9,10},{10,1... | collective-permute-start | bytes 6152 | tf_op jit(solution)/shard_map/ppermute | solution.py:11
  9.8 29.2 %copy-start.2 = (s32[16]{0:T(128)S(1)}, s32[16]{0:T(128)}, u32[]{:S(2)}) copy-start(s32[16]{0:T(128)} %param.11) | copy-start | bytes 196
  35.9 18.5 %collective-permute-start.1 = (bf16[127,2048]{1,0:T(8,128)(2,1)S(1)}, bf16[127,2048]{1,0:T(8,128)(2,1)S(1)}, u32[]{:S(2)}, u32[]{:S(2)}) collective-permute-start(bf16[127,2048]{1,0:T(8,128)(2,1)S(1)} %slice.62), channel_id=1, source_target_pairs={{0,16},{16,32},{32,48},{48,64},{64,80},{80,96},{96,112},{112,128},... | collective-permute-start | bytes 1560584 | tf_op jit(solution)/shard_map/ppermute | solution.py:11
where the time goes:
time: 98.5 us; the launch traced here: 97.9 us
  blocking collectives  43.6 us (44%)
  other arithmetic  15.7 us (16%)
  matrix products  14.2 us (14%)
  waiting for transfers between devices  11.8 us (12%)
  starting transfers between devices  7.67 us (8%)
  local copies, waits for them, and re-layouts  4.29 us (4%)
    all_gather x1, blocking collectives, on_device(): spectra = lax.all_gather(own_spectra, 'ir', axis=0, tiled=True)  22.5 us
    all_to_all x1, blocking collectives, sent_and_summed(): lax.all_to_all(tiles, axis, split_axis=0, concat_axis=0, tiled=True)  21.1 us
    ppermute x2, waiting for transfers between devices, from_behind(): return lax.ppermute(x, axis, pairs)  11.8 us
    convert_element_type x8, other arithmetic, add_partition(): chosen.astype(jnp.float32)  9.15 us
    ppermute x2, starting transfers between devices, from_behind(): return lax.ppermute(x, axis, pairs)  7.67 us
    dot_general x1, matrix products, on_device(): jnp.dot(summed, inverse, precision=lax.Precision.HIGHEST, preferred_eleme...  7.21 us
    dot_general x2, matrix products, on_device(): jnp.dot(frames, forward_table(width), preferred_element_type=jnp.float32)  5.72 us
    reshape x1, local copies, waits for them, and re-layouts, on_device(): selected = selected.reshape(count, part_dev, 2 * width)  2.23 us
  transfers between devices with their start and end apart: 2, of which 1 were waited for; matrix products, arithmetic and copies ran while one was open for 9% of the time, Pallas kernels for 0%

commit v1 on v0

--- a/solution.py
+++ b/solution.py
@@ -86,7 +86,29 @@
     begin, room = clip_info(clip_lengths, room_ids, blocks)
     room_hot = (room[:, None] == jnp.arange(rooms, dtype=jnp.int32)[None, :]).astype(jnp.bfloat16)
     inverse = inverse_table(width)
-    spectra = lax.all_gather(own_spectra, "ir", axis=0, tiled=True)
+    side_arr = lax.axis_size("ir")
+    then = lax.axis_index("ir")
+    newest, h_now, built = (side_arr, then, own_spectra.shape[0])
+    heap = tuple((i0 * newest if rr == 0 else i0 for rr, i0 in enumerate(own_spectra.shape)))
+    tmp = jnp.zeros(heap, own_spectra.dtype)
+    spectra = lax.dynamic_update_slice_in_dim(tmp, own_spectra, h_now * built, axis=0)
+    oldest = z_new = own_spectra
+    hop_no = 1
+    while hop_no < newest // 2 + 1:
+        oldest = lax.ppermute(
+            oldest, "ir", tuple(((rr, (rr + 1) % newest) for rr in range(newest)))
+        )
+        spectra = lax.dynamic_update_slice_in_dim(
+            spectra, oldest, (h_now - hop_no) % newest * built, axis=0
+        )
+        if 2 * hop_no < newest:
+            z_new = lax.ppermute(
+                z_new, "ir", tuple(((rr, (rr - 1) % newest) for rr in range(newest)))
+            )
+            spectra = lax.dynamic_update_slice_in_dim(
+                spectra, z_new, (h_now + hop_no) % newest * built, axis=0
+            )
+        hop_no = hop_no + 1
     delayed = from_behind(spectra[count - (parts - 1) :], "tile", 1)
     padded = jnp.concatenate([delayed, spectra], axis=0)
     flat_filters = ir_spectra.reshape(rooms, part_dev * 2 * width)

time: 98.5 us -> 114 us (1.16)
  starting transfers between devices: 7.67 us -> 33.8 us
  blocking collectives: 43.6 us -> 24.9 us
  waiting for transfers between devices: 11.8 us -> 19.1 us
    ppermute x0 -> x15, starting transfers between devices: none -> 27.3 us  [the longest x7 27.3 us: on_device(): lax.ppermute(z_new, 'ir', tuple(((rr, (rr - 1) % newest) for rr in range(...]
    all_gather x1 -> x0, blocking collectives: 22.5 us -> none  [on_device(): spectra = lax.all_gather(own_spectra, 'ir', axis=0, tiled=True)]
    ppermute x0 -> x15, waiting for transfers between devices: none -> 9.81 us  [the longest x8 8.67 us: on_device(): lax.ppermute(oldest, 'ir', tuple(((rr, (rr + 1) % newest) for rr in range...]
    all_to_all x1, blocking collectives: 21.1 us -> 24.9 us  [sent_and_summed(): lax.all_to_all(tiles, axis, split_axis=0, concat_axis=0, tiled=True)]
    ppermute x2, waiting for transfers between devices: 11.8 us -> 9.25 us  [from_behind(): return lax.ppermute(x, axis, pairs)]
    ppermute x2, starting transfers between devices: 7.67 us -> 6.47 us  [from_behind(): return lax.ppermute(x, axis, pairs)]
  transfers between devices with their start and end apart: 2 -> 17, of which waited for: 1 -> 16; matrix products, arithmetic and copies ran while one was open for 9% -> 8% of each run, Pallas kernels for 0% -> 0%
where the time goes in v1:
time: 114 us; the launch traced here: 113 us
  starting transfers between devices  33.8 us (30%)
  blocking collectives  24.9 us (22%)
  waiting for transfers between devices  19.1 us (17%)
  other arithmetic  15.8 us (14%)
  matrix products  14.3 us (13%)
  local copies, waits for them, and re-layouts  4.43 us (4%)
    ppermute x7, starting transfers between devices, on_device(): lax.ppermute(z_new, 'ir', tuple(((rr, (rr - 1) % newest) for rr in range(...  27.3 us
    all_to_all x1, blocking collectives, sent_and_summed(): lax.all_to_all(tiles, axis, split_axis=0, concat_axis=0, tiled=True)  24.9 us
    ppermute x2, waiting for transfers between devices, from_behind(): return lax.ppermute(x, axis, pairs)  9.25 us
    convert_element_type x8, other arithmetic, add_partition(): chosen.astype(jnp.float32)  9.15 us
    ppermute x8, waiting for transfers between devices, on_device(): lax.ppermute(oldest, 'ir', tuple(((rr, (rr + 1) % newest) for rr in range...  8.67 us
    dot_general x1, matrix products, on_device(): jnp.dot(summed, inverse, precision=lax.Precision.HIGHEST, preferred_eleme...  7.21 us
    ppermute x2, starting transfers between devices, from_behind(): return lax.ppermute(x, axis, pairs)  6.47 us
    dot_general x2, matrix products, on_device(): jnp.dot(frames, forward_table(width), preferred_element_type=jnp.float32)  5.78 us
  transfers between devices with their start and end apart: 17, of which 16 were waited for; matrix products, arithmetic and copies ran while one was open for 8% of the time, Pallas kernels for 0%

profile of v1, /device:TPU:33, one launch (start us, length us, event | category | flops | bytes accessed | tf_op | source)
XLA Modules:
  0.0 113.1 jit_solution(3745484852829365856)
XLA Ops:
  0.8 4.5 %collective-permute-start = (bf16[1,1024]{1,0:T(2,128)(2,1)S(1)}, bf16[1,1024]{1,0:T(2,128)(2,1)S(1)}, u32[]{:S(2)}, u32[]{:S(2)}) collective-permute-start(bf16[1,1024]{1,0:T(2,128)(2,1)S(1)} %slice.49), channel_id=1, source_target_pairs={{0,1},{1,2},{2,3},{3,4},{4,5},{5,6},{6,7},{7,8},{8,9},{9,10},{10,1... | collective-permute-start | bytes 6152 | tf_op jit(solution)/shard_map/ppermute | solution.py:11
  6.9 2.9 %convolution_bitcast_fusion = f32[8,2048]{1,0:T(8,128)S(1)} fusion(bf16[1024,2048]{1,0:T(8,128)(2,1)} %constant.206, bf16[8,1024]{1,0:T(8,128)(2,1)} %param.8), kind=kOutput, calls=%fused_computation.14 | convolution fusion | flops 33554432 | bytes 4276224 | tf_op jit(solution)/shard_map/dot_general | solution.py:82
  10.1 2.9 %constant_dynamic-update-slice_fusion.15 = (bf16[128,2048]{1,0:T(8,128)(2,1)S(1)}, bf16[8,2048]{1,0:T(8,128)(2,1)S(1)}) fusion(bf16[128,2048]{1,0:T(8,128)(2,1)S(1)} %broadcast_in_dim.83, s32[]{:T(128)S(6)} %select_n.159, f32[8,2048]{1,0:T(8,128)S(1)} %convolution_bitcast_fusion, bf16[1024,2048]{1,0:T(8,128)(2,1)} %constant.205, ...), kind=kOutput, calls=%fused_computation.45 | convolution fusion | flops 33628160 | bytes 4346372 | tf_op jit(solution)/shard_map/dot_general | solution.py:82
  13.0 5.2 %collective-permute-start.2 = (bf16[8,2048]{1,0:T(8,128)(2,1)S(1)}, bf16[8,2048]{1,0:T(8,128)(2,1)S(1)}, u32[]{:S(2)}, u32[]{:S(2)}) collective-permute-start(bf16[8,2048]{1,0:T(8,128)(2,1)S(1)} %get-tuple-element.249), channel_id=1, source_target_pairs={{0,15},{1,0},{2,1},{3,2},{4,3},{5,4},{6,5},{7,6},{8,7},{9,8},{10,9... | collective-permute-start | bytes 98312 | tf_op jit(solution)/shard_map/ppermute | solution.py:105
  19.0 3.7 %collective-permute-start.4 = (bf16[8,2048]{1,0:T(8,128)(2,1)S(1)}, bf16[8,2048]{1,0:T(8,128)(2,1)S(1)}, u32[]{:S(2)}, u32[]{:S(2)}) collective-permute-start(bf16[8,2048]{1,0:T(8,128)(2,1)S(1)} %collective-permute-done.2), channel_id=1, source_target_pairs={{0,15},{1,0},{2,1},{3,2},{4,3},{5,4},{6,5},{7,6},{8,7},{9,8},{10,9... | collective-permute-start | bytes 98312 | tf_op jit(solution)/shard_map/ppermute | solution.py:105
  23.6 3.7 %collective-permute-start.6 = (bf16[8,2048]{1,0:T(8,128)(2,1)S(1)}, bf16[8,2048]{1,0:T(8,128)(2,1)S(1)}, u32[]{:S(2)}, u32[]{:S(2)}) collective-permute-start(bf16[8,2048]{1,0:T(8,128)(2,1)S(1)} %collective-permute-done.4), channel_id=1, source_target_pairs={{0,15},{1,0},{2,1},{3,2},{4,3},{5,4},{6,5},{7,6},{8,7},{9,8},{10,9... | collective-permute-start | bytes 98312 | tf_op jit(solution)/shard_map/ppermute | solution.py:105
  28.1 3.7 %collective-permute-start.8 = (bf16[8,2048]{1,0:T(8,128)(2,1)S(1)}, bf16[8,2048]{1,0:T(8,128)(2,1)S(1)}, u32[]{:S(2)}, u32[]{:S(2)}) collective-permute-start(bf16[8,2048]{1,0:T(8,128)(2,1)S(1)} %collective-permute-done.6), channel_id=1, source_target_pairs={{0,15},{1,0},{2,1},{3,2},{4,3},{5,4},{6,5},{7,6},{8,7},{9,8},{10,9... | collective-permute-start | bytes 98312 | tf_op jit(solution)/shard_map/ppermute | solution.py:105
  32.7 3.7 %collective-permute-start.10 = (bf16[8,2048]{1,0:T(8,128)(2,1)S(1)}, bf16[8,2048]{1,0:T(8,128)(2,1)S(1)}, u32[]{:S(2)}, u32[]{:S(2)}) collective-permute-start(bf16[8,2048]{1,0:T(8,128)(2,1)S(1)} %collective-permute-done.8), channel_id=1, source_target_pairs={{0,15},{1,0},{2,1},{3,2},{4,3},{5,4},{6,5},{7,6},{8,7},{9,8},{10,9... | collective-permute-start | bytes 98312 | tf_op jit(solution)/shard_map/ppermute | solution.py:105
  37.2 3.7 %collective-permute-start.12 = (bf16[8,2048]{1,0:T(8,128)(2,1)S(1)}, bf16[8,2048]{1,0:T(8,128)(2,1)S(1)}, u32[]{:S(2)}, u32[]{:S(2)}) collective-permute-start(bf16[8,2048]{1,0:T(8,128)(2,1)S(1)} %collective-permute-done.10), channel_id=1, source_target_pairs={{0,15},{1,0},{2,1},{3,2},{4,3},{5,4},{6,5},{7,6},{8,7},{9,8},{10,9... | collective-permute-start | bytes 98312 | tf_op jit(solution)/shard_map/ppermute | solution.py:105
  41.8 3.7 %collective-permute-start.14 = (bf16[8,2048]{1,0:T(8,128)(2,1)S(1)}, bf16[8,2048]{1,0:T(8,128)(2,1)S(1)}, u32[]{:S(2)}, u32[]{:S(2)}) collective-permute-start(bf16[8,2048]{1,0:T(8,128)(2,1)S(1)} %collective-permute-done.12), channel_id=1, source_target_pairs={{0,15},{1,0},{2,1},{3,2},{4,3},{5,4},{6,5},{7,6},{8,7},{9,8},{10,9... | collective-permute-start | bytes 98312 | tf_op jit(solution)/shard_map/ppermute | solution.py:105
  46.3 4.4 %collective-permute-done.15 = bf16[8,2048]{1,0:T(8,128)(2,1)S(1)} collective-permute-done((bf16[8,2048]{1,0:T(8,128)(2,1)S(1)}, bf16[8,2048]{1,0:T(8,128)(2,1)S(1)}, u32[]{:S(2)}, u32[]{:S(2)}) %collective-permute-start.15) | collective-permute-done | bytes 32800 | tf_op jit(solution)/shard_map/ppermute | solution.py:98
  50.9 1.9 %collective-permute-start.16 = (bf16[127,2048]{1,0:T(8,128)(2,1)S(1)}, bf16[127,2048]{1,0:T(8,128)(2,1)S(1)}, u32[]{:S(2)}, u32[]{:S(2)}) collective-permute-start(bf16[127,2048]{1,0:T(8,128)(2,1)S(1)} %slice.62), channel_id=1, source_target_pairs={{0,16},{16,32},{32,48},{48,64},{64,80},{80,96},{96,112},{112,128},... | collective-permute-start | bytes 1560584 | tf_op jit(solution)/shard_map/ppermute | solution.py:11
  52.9 1.3 %convolution_convert_fusion = bf16[128,16384]{1,0:T(8,128)(2,1)S(1)} fusion(bf16[16,16384]{1,0:T(8,128)(2,1)S(1)} %reshape.73, s32[128]{0:T(128)S(1)} %get-tuple-element.230), kind=kOutput, calls=%fused_computation.12 | convolution fusion | flops 69208064 | bytes 4719104 | tf_op jit(solution)/shard_map/dot_general | solution.py:115
  54.2 2.3 %copy.15 = bf16[16,8,8,2048]{3,2,0,1:T(8,128)(2,1)} copy(bf16[16,8,8,2048]{3,2,1,0:T(8,128)(2,1)S(1)} %bitcast.21) | data formatting | bytes 8388608 | tf_op jit(solution)/shard_map/reshape | solution.py:118
  56.5 9.2 %collective-permute-done.16 = bf16[127,2048]{1,0:T(8,128)(2,1)S(1)} collective-permute-done((bf16[127,2048]{1,0:T(8,128)(2,1)S(1)}, bf16[127,2048]{1,0:T(8,128)(2,1)S(1)}, u32[]{:S(2)}, u32[]{:S(2)}) %collective-permute-start.16) | collective-permute-done | bytes 520224 | tf_op jit(solution)/shard_map/ppermute | solution.py:11
  65.9 14.5 %while.16 = (s32[]{:T(128)}, f32[128,2048]{1,0:T(8,128)S(1)}, s32[]{:T(128)}, s32[128]{0:T(128)S(1)}, bf16[255,2048]{1,0:T(8,128)(2,1)S(1)}, /*index=5*/bf16[128...) while((s32[]{:T(128)}, f32[128,2048]{1,0:T(8,128)S(1)}, ...), condition=%wide.region_5.6_spmd.clone, body=%wide.region_4.5_spmd.clone.sunk | while | flops 3020168 | bytes 9454529 | solution.py:129
  66.0 1.1 %bitcast_convert_fusion.2 = f32[128,2048]{1,0:T(8,128)S(1)} fusion(bf16[128,8,2048]{2,0,1:T(8,128)(2,1)} %get-tuple-element.324, s32[]{:T(128)} %get-tuple-element.308), kind=kLoop, calls=%fused_computation.3.clone.1 | loop fusion | flops 262144 | bytes 1572868 | tf_op jit(solution)/shard_map/while/body/eval_jaxpr/convert_element_type | solution.py:126
  67.8 1.1 %bitcast_convert_fusion.2 = f32[128,2048]{1,0:T(8,128)S(1)} fusion(bf16[128,8,2048]{2,0,1:T(8,128)(2,1)} %get-tuple-element.324, s32[]{:T(128)} %get-tuple-element.308), kind=kLoop, calls=%fused_computation.3.clone.1 | loop fusion | flops 262144 | bytes 1572868 | tf_op jit(solution)/shard_map/while/body/eval_jaxpr/convert_element_type | solution.py:126
  69.7 1.1 %bitcast_convert_fusion.2 = f32[128,2048]{1,0:T(8,128)S(1)} fusion(bf16[128,8,2048]{2,0,1:T(8,128)(2,1)} %get-tuple-element.324, s32[]{:T(128)} %get-tuple-element.308), kind=kLoop, calls=%fused_computation.3.clone.1 | loop fusion | flops 262144 | bytes 1572868 | tf_op jit(solution)/shard_map/while/body/eval_jaxpr/convert_element_type | solution.py:126
  71.5 1.1 %bitcast_convert_fusion.2 = f32[128,2048]{1,0:T(8,128)S(1)} fusion(bf16[128,8,2048]{2,0,1:T(8,128)(2,1)} %get-tuple-element.324, s32[]{:T(128)} %get-tuple-element.308), kind=kLoop, calls=%fused_computation.3.clone.1 | loop fusion | flops 262144 | bytes 1572868 | tf_op jit(solution)/shard_map/while/body/eval_jaxpr/convert_element_type | solution.py:126
  73.3 1.1 %bitcast_convert_fusion.2 = f32[128,2048]{1,0:T(8,128)S(1)} fusion(bf16[128,8,2048]{2,0,1:T(8,128)(2,1)} %get-tuple-element.324, s32[]{:T(128)} %get-tuple-element.308), kind=kLoop, calls=%fused_computation.3.clone.1 | loop fusion | flops 262144 | bytes 1572868 | tf_op jit(solution)/shard_map/while/body/eval_jaxpr/convert_element_type | solution.py:126
  78.7 1.1 %bitcast_convert_fusion.2 = f32[128,2048]{1,0:T(8,128)S(1)} fusion(bf16[128,8,2048]{2,0,1:T(8,128)(2,1)} %get-tuple-element.324, s32[]{:T(128)} %get-tuple-element.308), kind=kLoop, calls=%fused_computation.3.clone.1 | loop fusion | flops 262144 | bytes 1572868 | tf_op jit(solution)/shard_map/while/body/eval_jaxpr/convert_element_type | solution.py:126
  80.4 7.2 %convolution_bitcast_fusion.1 = f32[16,8,1024]{2,1,0:T(8,128)S(1)} fusion(f32[128,2048]{1,0:T(8,128)S(1)} %get-tuple-element.181, f32[2048,1024]{1,0:T(8,128)} %constant.201.clone), kind=kOutput, calls=%fused_computation.17 | convolution fusion | flops 3221225472 | bytes 9961472 | tf_op jit(solution)/shard_map/dot_general | solution.py:131
  87.6 24.9 %all_to_all.5 = f32[16,8,1024]{2,1,0:T(8,128)S(1)} all-to-all(f32[16,8,1024]{2,1,0:T(8,128)S(1)} %convolution_bitcast_fusion.1), channel_id=1, replica_groups=mesh['tile'=32,'ir'=16] {'ir'}, dimensions={0} | all-to-all | bytes 1048576 | tf_op jit(solution)/shard_map/all_to_all | solution.py:21
  (110 shorter events, 16.5 us)
Async XLA Ops:
  0.0 10.1 %copy-start.1 = (bf16[8,1024]{1,0:T(8,128)(2,1)S(1)}, bf16[8,1024]{1,0:T(8,128)(2,1)}, u32[]{:S(2)}) copy-start(bf16[8,1024]{1,0:T(8,128)(2,1)} %param.8) | copy-start | bytes 49156
  0.8 9.2 %collective-permute-start = (bf16[1,1024]{1,0:T(2,128)(2,1)S(1)}, bf16[1,1024]{1,0:T(2,128)(2,1)S(1)}, u32[]{:S(2)}, u32[]{:S(2)}) collective-permute-start(bf16[1,1024]{1,0:T(2,128)(2,1)S(1)} %slice.49), channel_id=1, source_target_pairs={{0,1},{1,2},{2,3},{3,4},{4,5},{5,6},{6,7},{7,8},{8,9},{9,10},{10,1... | collective-permute-start | bytes 6152 | tf_op jit(solution)/shard_map/ppermute | solution.py:11
  6.9 11.2 %copy-start = (bf16[16,8,2,1024]{3,2,1,0:T(2,128)(2,1)S(1)}, bf16[16,8,2,1024]{3,2,1,0:T(2,128)(2,1)}, u32[]{:S(2)}) copy-start(bf16[16,8,2,1024]{3,2,1,0:T(2,128)(2,1)} %param.9) | copy-start | bytes 1572868
  10.0 42.8 %copy-start.2 = (s32[16]{0:T(128)S(1)}, s32[16]{0:T(128)}, u32[]{:S(2)}) copy-start(s32[16]{0:T(128)} %param.11) | copy-start | bytes 196
  13.0 5.9 %collective-permute-start.1 = (bf16[8,2048]{1,0:T(8,128)(2,1)S(1)}, bf16[8,2048]{1,0:T(8,128)(2,1)S(1)}, u32[]{:S(2)}, u32[]{:S(2)}) collective-permute-start(bf16[8,2048]{1,0:T(8,128)(2,1)S(1)} %get-tuple-element.249), channel_id=1, source_target_pairs={{0,1},{1,2},{2,3},{3,4},{4,5},{5,6},{6,7},{7,8},{8,9},{9,10},{10,1... | collective-permute-start | bytes 98312 | tf_op jit(solution)/shard_map/ppermute | solution.py:98
  13.0 6.0 %collective-permute-start.2 = (bf16[8,2048]{1,0:T(8,128)(2,1)S(1)}, bf16[8,2048]{1,0:T(8,128)(2,1)S(1)}, u32[]{:S(2)}, u32[]{:S(2)}) collective-permute-start(bf16[8,2048]{1,0:T(8,128)(2,1)S(1)} %get-tuple-element.249), channel_id=1, source_target_pairs={{0,15},{1,0},{2,1},{3,2},{4,3},{5,4},{6,5},{7,6},{8,7},{9,8},{10,9... | collective-permute-start | bytes 98312 | tf_op jit(solution)/shard_map/ppermute | solution.py:105
  18.9 4.6 %collective-permute-start.3 = (bf16[8,2048]{1,0:T(8,128)(2,1)S(1)}, bf16[8,2048]{1,0:T(8,128)(2,1)S(1)}, u32[]{:S(2)}, u32[]{:S(2)}) collective-permute-start(bf16[8,2048]{1,0:T(8,128)(2,1)S(1)} %collective-permute-done.1), channel_id=1, source_target_pairs={{0,1},{1,2},{2,3},{3,4},{4,5},{5,6},{6,7},{7,8},{8,9},{9,10},{10,1... | collective-permute-start | bytes 98312 | tf_op jit(solution)/shard_map/ppermute | solution.py:98
  19.0 4.6 %collective-permute-start.4 = (bf16[8,2048]{1,0:T(8,128)(2,1)S(1)}, bf16[8,2048]{1,0:T(8,128)(2,1)S(1)}, u32[]{:S(2)}, u32[]{:S(2)}) collective-permute-start(bf16[8,2048]{1,0:T(8,128)(2,1)S(1)} %collective-permute-done.2), channel_id=1, source_target_pairs={{0,15},{1,0},{2,1},{3,2},{4,3},{5,4},{6,5},{7,6},{8,7},{9,8},{10,9... | collective-permute-start | bytes 98312 | tf_op jit(solution)/shard_map/ppermute | solution.py:105
  23.4 4.6 %collective-permute-start.5 = (bf16[8,2048]{1,0:T(8,128)(2,1)S(1)}, bf16[8,2048]{1,0:T(8,128)(2,1)S(1)}, u32[]{:S(2)}, u32[]{:S(2)}) collective-permute-start(bf16[8,2048]{1,0:T(8,128)(2,1)S(1)} %collective-permute-done.3), channel_id=1, source_target_pairs={{0,1},{1,2},{2,3},{3,4},{4,5},{5,6},{6,7},{7,8},{8,9},{9,10},{10,1... | collective-permute-start | bytes 98312 | tf_op jit(solution)/shard_map/ppermute | solution.py:98
  23.6 4.6 %collective-permute-start.6 = (bf16[8,2048]{1,0:T(8,128)(2,1)S(1)}, bf16[8,2048]{1,0:T(8,128)(2,1)S(1)}, u32[]{:S(2)}, u32[]{:S(2)}) collective-permute-start(bf16[8,2048]{1,0:T(8,128)(2,1)S(1)} %collective-permute-done.4), channel_id=1, source_target_pairs={{0,15},{1,0},{2,1},{3,2},{4,3},{5,4},{6,5},{7,6},{8,7},{9,8},{10,9... | collective-permute-start | bytes 98312 | tf_op jit(solution)/shard_map/ppermute | solution.py:105
  28.0 4.6 %collective-permute-start.7 = (bf16[8,2048]{1,0:T(8,128)(2,1)S(1)}, bf16[8,2048]{1,0:T(8,128)(2,1)S(1)}, u32[]{:S(2)}, u32[]{:S(2)}) collective-permute-start(bf16[8,2048]{1,0:T(8,128)(2,1)S(1)} %collective-permute-done.5), channel_id=1, source_target_pairs={{0,1},{1,2},{2,3},{3,4},{4,5},{5,6},{6,7},{7,8},{8,9},{9,10},{10,1... | collective-permute-start | bytes 98312 | tf_op jit(solution)/shard_map/ppermute | solution.py:98
  28.1 4.6 %collective-permute-start.8 = (bf16[8,2048]{1,0:T(8,128)(2,1)S(1)}, bf16[8,2048]{1,0:T(8,128)(2,1)S(1)}, u32[]{:S(2)}, u32[]{:S(2)}) collective-permute-start(bf16[8,2048]{1,0:T(8,128)(2,1)S(1)} %collective-permute-done.6), channel_id=1, source_target_pairs={{0,15},{1,0},{2,1},{3,2},{4,3},{5,4},{6,5},{7,6},{8,7},{9,8},{10,9... | collective-permute-start | bytes 98312 | tf_op jit(solution)/shard_map/ppermute | solution.py:105
  32.5 4.6 %collective-permute-start.9 = (bf16[8,2048]{1,0:T(8,128)(2,1)S(1)}, bf16[8,2048]{1,0:T(8,128)(2,1)S(1)}, u32[]{:S(2)}, u32[]{:S(2)}) collective-permute-start(bf16[8,2048]{1,0:T(8,128)(2,1)S(1)} %collective-permute-done.7), channel_id=1, source_target_pairs={{0,1},{1,2},{2,3},{3,4},{4,5},{5,6},{6,7},{7,8},{8,9},{9,10},{10,1... | collective-permute-start | bytes 98312 | tf_op jit(solution)/shard_map/ppermute | solution.py:98
  32.7 4.6 %collective-permute-start.10 = (bf16[8,2048]{1,0:T(8,128)(2,1)S(1)}, bf16[8,2048]{1,0:T(8,128)(2,1)S(1)}, u32[]{:S(2)}, u32[]{:S(2)}) collective-permute-start(bf16[8,2048]{1,0:T(8,128)(2,1)S(1)} %collective-permute-done.8), channel_id=1, source_target_pairs={{0,15},{1,0},{2,1},{3,2},{4,3},{5,4},{6,5},{7,6},{8,7},{9,8},{10,9... | collective-permute-start | bytes 98312 | tf_op jit(solution)/shard_map/ppermute | solution.py:105
  37.1 4.6 %collective-permute-start.11 = (bf16[8,2048]{1,0:T(8,128)(2,1)S(1)}, bf16[8,2048]{1,0:T(8,128)(2,1)S(1)}, u32[]{:S(2)}, u32[]{:S(2)}) collective-permute-start(bf16[8,2048]{1,0:T(8,128)(2,1)S(1)} %collective-permute-done.9), channel_id=1, source_target_pairs={{0,1},{1,2},{2,3},{3,4},{4,5},{5,6},{6,7},{7,8},{8,9},{9,10},{10,1... | collective-permute-start | bytes 98312 | tf_op jit(solution)/shard_map/ppermute | solution.py:98
  37.2 4.6 %collective-permute-start.12 = (bf16[8,2048]{1,0:T(8,128)(2,1)S(1)}, bf16[8,2048]{1,0:T(8,128)(2,1)S(1)}, u32[]{:S(2)}, u32[]{:S(2)}) collective-permute-start(bf16[8,2048]{1,0:T(8,128)(2,1)S(1)} %collective-permute-done.10), channel_id=1, source_target_pairs={{0,15},{1,0},{2,1},{3,2},{4,3},{5,4},{6,5},{7,6},{8,7},{9,8},{10,9... | collective-permute-start | bytes 98312 | tf_op jit(solution)/shard_map/ppermute | solution.py:105
  41.6 4.6 %collective-permute-start.13 = (bf16[8,2048]{1,0:T(8,128)(2,1)S(1)}, bf16[8,2048]{1,0:T(8,128)(2,1)S(1)}, u32[]{:S(2)}, u32[]{:S(2)}) collective-permute-start(bf16[8,2048]{1,0:T(8,128)(2,1)S(1)} %collective-permute-done.11), channel_id=1, source_target_pairs={{0,1},{1,2},{2,3},{3,4},{4,5},{5,6},{6,7},{7,8},{8,9},{9,10},{10,1... | collective-permute-start | bytes 98312 | tf_op jit(solution)/shard_map/ppermute | solution.py:98
  41.8 4.6 %collective-permute-start.14 = (bf16[8,2048]{1,0:T(8,128)(2,1)S(1)}, bf16[8,2048]{1,0:T(8,128)(2,1)S(1)}, u32[]{:S(2)}, u32[]{:S(2)}) collective-permute-start(bf16[8,2048]{1,0:T(8,128)(2,1)S(1)} %collective-permute-done.12), channel_id=1, source_target_pairs={{0,15},{1,0},{2,1},{3,2},{4,3},{5,4},{6,5},{7,6},{8,7},{9,8},{10,9... | collective-permute-start | bytes 98312 | tf_op jit(solution)/shard_map/ppermute | solution.py:105
  46.2 4.6 %collective-permute-start.15 = (bf16[8,2048]{1,0:T(8,128)(2,1)S(1)}, bf16[8,2048]{1,0:T(8,128)(2,1)S(1)}, u32[]{:S(2)}, u32[]{:S(2)}) collective-permute-start(bf16[8,2048]{1,0:T(8,128)(2,1)S(1)} %collective-permute-done.13), channel_id=1, source_target_pairs={{0,1},{1,2},{2,3},{3,4},{4,5},{5,6},{6,7},{7,8},{8,9},{9,10},{10,1... | collective-permute-start | bytes 98312 | tf_op jit(solution)/shard_map/ppermute | solution.py:98
  50.9 14.8 %collective-permute-start.16 = (bf16[127,2048]{1,0:T(8,128)(2,1)S(1)}, bf16[127,2048]{1,0:T(8,128)(2,1)S(1)}, u32[]{:S(2)}, u32[]{:S(2)}) collective-permute-start(bf16[127,2048]{1,0:T(8,128)(2,1)S(1)} %slice.62), channel_id=1, source_target_pairs={{0,16},{16,32},{32,48},{48,64},{64,80},{80,96},{96,112},{112,128},... | collective-permute-start | bytes 1560584 | tf_op jit(solution)/shard_map/ppermute | solution.py:11
